TPU v7x, 32 devices: a whole 2x2x4 slice. The times are simulated.
32 devices in a mesh: section: 2 (over core), rep: 4 (over z), expert: 4 (over y, x).
Axes of the slice: x: 2, y: 2, z: 4, core: 2. Of those that a mesh axis runs over, the one named last changes fastest.
Arguments:
- activations: bfloat16 [2, 4, 256, 7168], P('section', 'rep', 'expert'), may hold values from -6 to 6
- routes: int32 [2, 4, 256, 8], P('section', 'rep', 'expert'), may hold values from 0 to 255, all different within a row; in each aligned block of 64 rows (0 to 63, 64 to 127, ..., all dimensions but the last counted through in order) at most 2 rows name the same one
- gate_values: float32 [2, 4, 256, 8], P('section', 'rep', 'expert'), may hold values from 0.1 to 1
- w_gate: bfloat16 [2, 7168, 8192], P('section', None, 'expert'), may hold values from -0.0625 to 0.0625
- w_up: bfloat16 [2, 7168, 8192], P('section', None, 'expert'), may hold values from -0.0625 to 0.0625
- w_down: bfloat16 [2, 8192, 7168], P('section', 'expert'), may hold values from -0.125 to 0.125
Outputs:
- handed: bfloat16 [2, 4, 256, 7168], P('section', 'rep', 'expert')
- load_share: float32 [2, 4], P('section')
Inputs may be any that keep to these rules, and one draw needn't show every extreme that they name: The 8 routes of a token name different experts; in each aligned block of 64 tokens (the tokens of one device) at most 2 tokens name one expert.
All inputs are finite; a program needn't handle non-finite values.
Results may differ from a plain program's by a relative error of at most 0.012.
Values may be sent and summed in bfloat16 or wider, within the bound.
No kernel may reach another device: no remote copies, remote signals or barrier semaphores. Data moves between devices by JAX's collectives and lax.ppermute only.
A program may use at most 128 MiB of HBM per device.

v0:
```python
import jax
import jax.numpy as jnp
from jax import lax
from jax.sharding import PartitionSpec as P

EXPERTS = 4
CAPACITY = 2


def from_behind(block, axis, distance):
    devices = range(lax.axis_size(axis))
    route = [((i - distance) % len(devices), i) for i in devices]
    return lax.ppermute(block, axis, route)


def route_tables(route_ids, gates):
    expert_ids = jnp.arange(EXPERTS, dtype=jnp.int32)
    matches = (route_ids[:, :, None] == expert_ids[None, None, :]).astype(jnp.float32)
    hits = jnp.sum(matches, axis=1)
    mass = jnp.sum(gates[:, :, None] * matches, axis=1)
    return (hits, mass)


def slot_picks(hits):
    before = jnp.cumsum(hits, axis=0) - hits
    slots = jnp.arange(CAPACITY).astype(jnp.float32)
    picks = hits[:, :, None] * (before[:, :, None] == slots[None, None, :]).astype(jnp.float32)
    return jnp.transpose(picks, (1, 2, 0))


def local(activations, routes, gate_values, w_gate, w_up, w_down):
    peers = lax.axis_size("expert")
    members = peers // EXPERTS
    highest = lax.Precision.HIGHEST
    rows_here = activations[0, 0]
    tok_here = rows_here.shape[0]
    width = rows_here.shape[1]
    hits, gate_mass = route_tables(routes[0, 0], gate_values[0, 0])
    slot_weights = gate_mass.astype(jnp.bfloat16)
    picks = slot_picks(hits)
    buffer = jnp.einsum(
        "ect,td->ecd", picks.astype(jnp.bfloat16), rows_here, preferred_element_type=jnp.float32
    ).astype(jnp.bfloat16)
    buffer_weights = jnp.einsum(
        "ect,te->ec", picks, slot_weights.astype(jnp.float32), precision=highest
    )
    copies = jnp.repeat(buffer, members, axis=0)
    copy_weights = jnp.repeat(buffer_weights, members, axis=0).astype(jnp.bfloat16)
    gate_w = w_gate[0]
    up_w = w_up[0]
    down_w = w_down[0]
    got_rows, got_weights = (
        lax.all_to_all(copies, "expert", split_axis=0, concat_axis=0, tiled=True),
        lax.all_to_all(copy_weights, "expert", split_axis=0, concat_axis=0, tiled=True),
    )
    sources = got_rows.shape[0]
    slots = got_rows.shape[1]
    flat = got_rows.reshape(sources * slots, width)
    gate_proj = jnp.dot(flat, gate_w, preferred_element_type=jnp.float32)
    up_proj = jnp.dot(flat, up_w, preferred_element_type=jnp.float32)
    hidden = (jax.nn.silu(gate_proj) * up_proj).astype(jnp.bfloat16)
    partial_out = jnp.dot(hidden, down_w, preferred_element_type=jnp.float32)
    scale = got_weights.reshape(sources * slots).astype(jnp.float32)
    weighted = (scale[:, None] * partial_out).astype(jnp.bfloat16)
    weighted = weighted.reshape(sources, slots, width)
    returned = lax.all_to_all(weighted, "expert", split_axis=0, concat_axis=0, tiled=True)
    per_expert = jnp.sum(
        returned.astype(jnp.float32).reshape(EXPERTS, members, CAPACITY, width), axis=1
    )
    mixed = jnp.einsum("ect,ecd->td", picks, per_expert, precision=highest).astype(jnp.bfloat16)
    handed = from_behind(mixed, "section", 1)
    total_load = lax.psum(jnp.sum(gate_mass, axis=0), ("rep", "expert"))
    load_share = total_load / jnp.float32(lax.axis_size("rep") * peers * tok_here)
    return (handed[None, None], load_share[None])


def solution(mesh):
    placed = (
        P("section", "rep", "expert", None),
        P("section", "rep", "expert", None),
        P("section", "rep", "expert", None),
        P("section", None, "expert"),
        P("section", None, "expert"),
        P("section", "expert", None),
    )
    return jax.shard_map(
        local,
        mesh=mesh,
        in_specs=placed,
        out_specs=(P("section", "rep", "expert", None), P("section", None)),
        check_vma=False,
    )
```

profile of v0, /device:TPU:0, one launch (start us, length us, event | category | flops | bytes accessed | tf_op | source)
XLA Modules:
  0.0 102.7 jit_solution(6931539595291845301)
XLA Ops:
  0.6 0.0 copy-start
  0.7 0.9 select_reduce_fusion
  1.6 0.1 copy.28
  1.6 0.1 copy.31
  1.7 0.1 reduce_window_sum.13
  1.8 0.1 copy.30
  1.9 0.1 compare_select_fusion
  2.0 0.1 fusion.29
  2.1 0.1 copy.37
  2.2 0.7 copy.32
  3.0 5.2 %all-to-all-start = ((bf16[4,1,2]{2,1,0:T(2,128)(2,1)}), bf16[4,1,2]{2,1,0:T(2,128)(2,1)S(1)}, u32[]{:S(2)}, u32[]{:S(2)}) async-start(bf16[4,1,2]{2,1,0:T(2,128)(2,1)} %copy.32), calls=%async_computation | async-start | bytes 4096 | tf_op jit(solution)/shard_map/all_to_all | solution.py:54
  8.1 0.0 copy-done
  8.1 0.3 convolution_convert_fusion
  8.4 0.7 copy.33
  9.2 3.5 %all-to-all-done = bf16[4,1,2]{2,1,0:T(2,128)(2,1)S(1)} async-done(((bf16[4,1,2]{2,1,0:T(2,128)(2,1)}), bf16[4,1,2]{2,1,0:T(2,128)(2,1)S(1)}, u32[]{:S(2)}, u32[]{:S(2)}) %all-to-all-start) | async-done | bytes 48 | tf_op jit(solution)/shard_map/all_to_all | solution.py:54
  12.7 3.3 %all-to-all-start.1 = ((bf16[4,2,7168]{2,1,0:T(2,128)(2,1)}), bf16[4,2,7168]{2,1,0:T(2,128)(2,1)S(1)}, u32[]{:S(2)}, u32[]{:S(2)}) async-start(bf16[4,2,7168]{2,1,0:T(2,128)(2,1)} %copy.33), calls=%async_computation.1 | async-start | bytes 229376 | tf_op jit(solution)/shard_map/all_to_all | solution.py:53
  16.0 0.1 reshape.42
  16.1 4.8 %all-to-all-done.1 = bf16[4,2,7168]{2,1,0:T(2,128)(2,1)S(1)} async-done(((bf16[4,2,7168]{2,1,0:T(2,128)(2,1)}), bf16[4,2,7168]{2,1,0:T(2,128)(2,1)S(1)}, u32[]{:S(2)}, u32[]{:S(2)}) %all-to-all-start.1) | async-done | bytes 114720 | tf_op jit(solution)/shard_map/all_to_all | solution.py:53
  21.0 11.4 %fusion.4 = f32[8,2048]{1,0:T(8,128)S(1)} fusion(bf16[8,7168]{1,0:T(8,128)(2,1)S(1)} %reshape.40, bf16[1,7168,2048]{2,1,0:T(8,128)(2,1)} %param.9), kind=kOutput, calls=%fused_computation.4 | convolution fusion | flops 234881024 | bytes 29540352 | tf_op jit(solution)/shard_map/dot_general | solution.py:59
  32.3 20.1 %fusion.10 = bf16[8,7168]{1,0:T(8,128)(2,1)S(1)} fusion(bf16[1,2048,7168]{2,1,0:T(8,128)(2,1)} %param.11, bf16[8,7168]{1,0:T(8,128)(2,1)S(1)} %reshape.40, bf16[1,7168,2048]{2,1,0:T(8,128)(2,1)} %param.10, f32[8]{0:T(128)S(1)} %reshape.42, f32[8,2048]{1,0:T(8,128)S(1)} %fusion.4), kind=kOutput, calls=%fused_computation.9 | convolution fusion | flops 469975040 | bytes 59015200 | tf_op jit(solution)/shard_map/dot_general | solution.py:62
  52.5 7.4 %all_to_all.19 = bf16[4,2,7168]{2,1,0:T(2,128)(2,1)S(1)} all-to-all(bf16[4,2,7168]{2,1,0:T(2,128)(2,1)S(1)} %reshape.41), channel_id=1, replica_groups=mesh['section'=2,'rep'=4,'expert'=4] {'expert'}, dimensions={0} | all-to-all | bytes 229376 | tf_op jit(solution)/shard_map/all_to_all | solution.py:66
  59.9 1.0 %fusion.6 = bf16[64,7168]{1,0:T(8,128)(2,1)S(1)} fusion(bf16[4,2,7168]{2,1,0:T(2,128)(2,1)S(1)} %all_to_all.19, f32[4,64]{1,0:T(4,128)S(1)} %copy.31, f32[4,64]{1,0:T(4,128)S(1)} %copy.30, f32[2]{0:T(128)S(1)} %iota_convert_fusion), kind=kOutput, calls=%fused_computation.7 | convolution fusion | flops 44499968 | bytes 1034248 | tf_op jit(solution)/shard_map/ect,ecd->td/dot_general | solution.py:70
  60.9 0.1 collective-permute-start
  61.0 40.2 %psum.7 = f32[4]{0:T(128)S(1)} all-reduce(f32[4]{0:T(128)S(1)} %get-tuple-element.2), channel_id=1, replica_groups=mesh['section'=2,'rep'=4,'expert'=4] {'rep','expert'}, use_global_device_ids=true, to_apply=%region_4.5 | all-reduce | flops 4 | bytes 32 | tf_op jit(solution)/shard_map/psum | solution.py:72
  101.2 0.5 multiply_bitcast_fusion
  101.7 0.0 collective-permute-done
  101.7 0.9 copy.45
  (6 shorter events, 0.1 us)
Async XLA Ops:
  0.6 7.5 %copy-start = (bf16[1,1,64,7168]{3,2,1,0:T(8,128)(2,1)S(1)}, bf16[1,1,64,7168]{3,2,1,0:T(8,128)(2,1)}, u32[]{:S(2)}) copy-start(bf16[1,1,64,7168]{3,2,1,0:T(8,128)(2,1)} %param.6) | copy-start | bytes 2752516
  3.0 9.7 %all-to-all-start = ((bf16[4,1,2]{2,1,0:T(2,128)(2,1)}), bf16[4,1,2]{2,1,0:T(2,128)(2,1)S(1)}, u32[]{:S(2)}, u32[]{:S(2)}) async-start(bf16[4,1,2]{2,1,0:T(2,128)(2,1)} %copy.32), calls=%async_computation | async-start | bytes 4096 | tf_op jit(solution)/shard_map/all_to_all | solution.py:54
  12.7 8.3 %all-to-all-start.1 = ((bf16[4,2,7168]{2,1,0:T(2,128)(2,1)}), bf16[4,2,7168]{2,1,0:T(2,128)(2,1)S(1)}, u32[]{:S(2)}, u32[]{:S(2)}) async-start(bf16[4,2,7168]{2,1,0:T(2,128)(2,1)} %copy.33), calls=%async_computation.1 | async-start | bytes 229376 | tf_op jit(solution)/shard_map/all_to_all | solution.py:53
  60.9 40.8 %collective-permute-start = (bf16[64,7168]{1,0:T(8,128)(2,1)S(1)}, bf16[64,7168]{1,0:T(8,128)(2,1)S(1)}, u32[]{:S(2)}, u32[]{:S(2)}) collective-permute-start(bf16[64,7168]{1,0:T(8,128)(2,1)S(1)} %fusion.6), channel_id=1, source_target_pairs={{16,0},{0,16},{17,1},{1,17},{18,2},{2,18},{19,3},{3,19},{20,4},{4,... | collective-permute-start | bytes 2752520 | tf_op jit(solution)/shard_map/ppermute | solution.py:13
where the time goes:
time: 103 us
  blocking collectives  47.6 us (46%)
  matrix products  33 us (32%)
  starting transfers between devices  8.58 us (8%)
  waiting for transfers between devices  8.32 us (8%)
  local copies, waits for them, and re-layouts  2.92 us (3%)
  other arithmetic  1.61 us (2%)
    psum x1, blocking collectives, local(): total_load = lax.psum(jnp.sum(gate_mass, axis=0), ('rep', 'expert'))  40.2 us
    dot_general x1, matrix products, local(): partial_out = jnp.dot(hidden, down_w, preferred_element_type=jnp.float32)  20.1 us
    dot_general x1, matrix products, local(): gate_proj = jnp.dot(flat, gate_w, preferred_element_type=jnp.float32)  11.4 us
    all_to_all x1, blocking collectives, local(): lax.all_to_all(weighted, 'expert', split_axis=0, concat_axis=0, tiled=True)  7.36 us
    all_to_all x1, starting transfers between devices, local(): lax.all_to_all(copy_weights, 'expert', split_axis=0, concat_axis=0, tiled...  5.19 us
    all_to_all x1, waiting for transfers between devices, local(): lax.all_to_all(copies, 'expert', split_axis=0, concat_axis=0, tiled=True)  4.84 us
    all_to_all x1, waiting for transfers between devices, local(): lax.all_to_all(copy_weights, 'expert', split_axis=0, concat_axis=0, tiled...  3.48 us
    all_to_all x1, starting transfers between devices, local(): lax.all_to_all(copies, 'expert', split_axis=0, concat_axis=0, tiled=True)  3.32 us
  transfers between devices with their start and end apart: 3, of which 2 were waited for; matrix products, arithmetic and copies ran while one was open for 2% of the time, Pallas kernels for 0%

commit v1 on v0

v1 whole, which is shorter than its diff:
```python
import functools

import jax
import jax.numpy as jnp
from jax import lax
from jax.experimental import pallas as pl
from jax.experimental.pallas import tpu as pltpu
from jax.sharding import PartitionSpec as P

EXPERTS = 4
CAPACITY = 2
BF16 = jnp.bfloat16
F32 = jnp.float32
ANY = pl.BlockSpec(memory_space=pl.ANY)
VMEM = pl.BlockSpec(memory_space=pltpu.VMEM)
SMEM = pl.BlockSpec(memory_space=pltpu.SMEM)


def partner(index, distance, count):
    if count & (count - 1) == 0:
        return index ^ distance
    return (index + distance) % count


def largest_chunk(total, limit, unit):
    best = unit
    for size in range(unit, min(total, limit) + 1, unit):
        if total % size == 0:
            best = size
    return best


def route_kernel(peers, members, me_ref, routes_ref, gates_ref, acts_ref, *refs):
    row_refs, picks_ref, mass_ref = refs[:peers], refs[peers], refs[peers + 1]
    me = me_ref[0]
    routes = routes_ref[...]
    gates = gates_ref[...]
    tokens = routes.shape[1]
    hits, mass = [], []
    for expert in range(EXPERTS):
        match = routes == expert
        hits.append(jnp.sum(jnp.where(match, 1.0, 0.0), axis=0, keepdims=True))
        mass.append(jnp.sum(jnp.where(match, gates, 0.0), axis=0, keepdims=True))
    hits = jnp.concatenate(hits, axis=0)
    mass = jnp.concatenate(mass, axis=0)
    mass_ref[...] = jnp.broadcast_to(jnp.sum(mass, axis=1, keepdims=True), mass_ref.shape)
    earlier = lax.broadcasted_iota(jnp.int32, (tokens, tokens), 0) < lax.broadcasted_iota(
        jnp.int32, (tokens, tokens), 1
    )
    before = jnp.dot(hits, jnp.where(earlier, 1.0, 0.0), preferred_element_type=F32)
    weights = mass.astype(BF16).astype(F32)
    picks, scaled = [], []
    for distance in range(peers):
        expert = partner(me, distance, peers) // members
        chosen = lax.broadcasted_iota(jnp.int32, hits.shape, 0) == expert
        hit = jnp.sum(jnp.where(chosen, hits, 0.0), axis=0, keepdims=True)
        seen = jnp.sum(jnp.where(chosen, before, 0.0), axis=0, keepdims=True)
        weight = jnp.sum(jnp.where(chosen, weights, 0.0), axis=0, keepdims=True)
        for slot in range(CAPACITY):
            pick = jnp.where(seen == slot, hit, 0.0)
            picks.append(pick)
            scaled.append(pick * weight)
    picks = jnp.concatenate(picks, axis=0)
    picks_ref[...] = jnp.concatenate(scaled, axis=0).astype(BF16)
    rows = jnp.dot(picks.astype(BF16), acts_ref[...], preferred_element_type=F32).astype(BF16)
    for distance in range(peers):
        row_refs[distance][...] = rows[distance * CAPACITY : (distance + 1) * CAPACITY]


def expert_kernel(peers, depth, span, slots, *refs):
    row_refs = refs[:peers]
    gate_ref, up_ref, down_ref = refs[peers : peers + 3]
    out_refs = refs[peers + 3 : 2 * peers + 3]
    gate_buf, up_buf, down_buf, rows_ref, gate_sem, up_sem, down_sem = refs[2 * peers + 3 :]
    width, hidden = gate_ref.shape
    steps, pieces = width // depth, width // span
    down_slots = down_buf.shape[0]

    def first(ref, buf, sem, step):
        return pltpu.make_async_copy(
            ref.at[pl.ds(step * depth, depth), :], buf.at[step % slots], sem.at[step % slots]
        )

    def second(piece):
        return pltpu.make_async_copy(
            down_ref.at[:, pl.ds(piece * span, span)],
            down_buf.at[piece % down_slots],
            down_sem.at[piece % down_slots],
        )

    for step in range(min(slots, steps)):
        first(gate_ref, gate_buf, gate_sem, step).start()
        first(up_ref, up_buf, up_sem, step).start()
    for piece in range(min(down_slots, pieces)):
        second(piece).start()
    rows_ref[...] = jnp.concatenate([ref[...].astype(F32) for ref in row_refs], axis=0).astype(BF16)
    rows = rows_ref.shape[0]
    gate = jnp.zeros((rows, hidden), F32)
    up = jnp.zeros((rows, hidden), F32)
    for step in range(steps):
        first(gate_ref, gate_buf, gate_sem, step).wait()
        first(up_ref, up_buf, up_sem, step).wait()
        part = rows_ref[:, step * depth : (step + 1) * depth]
        gate = gate + jnp.dot(part, gate_buf[step % slots], preferred_element_type=F32)
        up = up + jnp.dot(part, up_buf[step % slots], preferred_element_type=F32)
        if step + slots < steps:
            first(gate_ref, gate_buf, gate_sem, step + slots).start()
            first(up_ref, up_buf, up_sem, step + slots).start()
    inner = (gate / (1.0 + jnp.exp(-gate)) * up).astype(BF16)
    for piece in range(pieces):
        second(piece).wait()
        result = jnp.dot(inner, down_buf[piece % down_slots], preferred_element_type=F32)
        result = result.astype(BF16)
        for source in range(peers):
            out_refs[source][:, piece * span : (piece + 1) * span] = result[
                source * CAPACITY : (source + 1) * CAPACITY
            ]
        if piece + down_slots < pieces:
            second(piece + down_slots).start()


def combine_kernel(peers, picks_ref, *refs):
    row_refs, out_ref = refs[:peers], refs[peers]
    rows = jnp.concatenate([ref[...].astype(F32) for ref in row_refs], axis=0).astype(BF16)
    out_ref[...] = lax.dot_general(
        picks_ref[...], rows, (((0,), (0,)), ((), ())), preferred_element_type=F32
    ).astype(BF16)


def local(activations, routes, gate_values, w_gate, w_up, w_down):
    peers = lax.axis_size("expert")
    sections = lax.axis_size("section")
    reps = lax.axis_size("rep")
    members = peers // EXPERTS
    tokens, width = activations.shape[2:]
    hidden = w_gate.shape[2]
    me = lax.axis_index("expert").astype(jnp.int32).reshape(1)
    rows_shape = jax.ShapeDtypeStruct((CAPACITY, width), BF16)
    *sent, picks, mass = pl.pallas_call(
        functools.partial(route_kernel, peers, members),
        out_shape=[rows_shape] * peers
        + [
            jax.ShapeDtypeStruct((peers * CAPACITY, tokens), BF16),
            jax.ShapeDtypeStruct((EXPERTS, 128), F32),
        ],
        in_specs=[SMEM, VMEM, VMEM, VMEM],
        out_specs=[VMEM] * (peers + 2),
        compiler_params=pltpu.CompilerParams(vmem_limit_bytes=8 << 20),
        name="route",
    )(me, routes[0, 0].T, gate_values[0, 0].T, activations[0, 0])

    order = sorted(range(1, peers), key=lambda d: -bin(d).count("1"))
    got = [sent[0]] + [None] * (peers - 1)
    for distance in order:
        route = [(i, partner(i, distance, peers)) for i in range(peers)]
        got[distance] = lax.ppermute(sent[distance], "expert", route)
    onward = [(s, (s + 1) % sections) for s in range(sections)]
    picks = lax.ppermute(picks, "section", onward)

    total = mass[:, :1]
    for axis, count in (("expert", peers), ("rep", reps)):
        reach = 1
        while reach < count:
            route = [(i, i ^ reach) for i in range(count)]
            total = total + lax.ppermute(total, axis, route)
            reach *= 2

    depth = largest_chunk(width, 512, 128)
    span = largest_chunk(width, 512, 128)
    back = pl.pallas_call(
        functools.partial(expert_kernel, peers, depth, span, 4),
        out_shape=[rows_shape] * peers,
        in_specs=[VMEM] * peers + [ANY] * 3,
        out_specs=[VMEM] * peers,
        scratch_shapes=[
            pltpu.VMEM((4, depth, hidden), BF16),
            pltpu.VMEM((4, depth, hidden), BF16),
            pltpu.VMEM((4, hidden, span), BF16),
            pltpu.VMEM((peers * CAPACITY, width), BF16),
            pltpu.SemaphoreType.DMA((4,)),
            pltpu.SemaphoreType.DMA((4,)),
            pltpu.SemaphoreType.DMA((4,)),
        ],
        compiler_params=pltpu.CompilerParams(vmem_limit_bytes=40 << 20),
        name="expert",
    )(*got, w_gate[0], w_up[0], w_down[0])

    home = [None] * peers
    for distance in order + [0]:
        route = [
            (s * peers + partner(i, distance, peers), (s + 1) % sections * peers + i)
            for s in range(sections)
            for i in range(peers)
        ]
        home[distance] = lax.ppermute(back[distance], ("section", "expert"), route)
    handed = pl.pallas_call(
        functools.partial(combine_kernel, peers),
        out_shape=jax.ShapeDtypeStruct((tokens, width), BF16),
        in_specs=[VMEM] * (peers + 1),
        out_specs=VMEM,
        compiler_params=pltpu.CompilerParams(vmem_limit_bytes=16 << 20),
        name="combine",
    )(picks, *home)
    load_share = total[:, 0] / F32(reps * peers * tokens)
    return (handed[None, None], load_share[None])


def solution(mesh):
    placed = (
        P("section", "rep", "expert", None),
        P("section", "rep", "expert", None),
        P("section", "rep", "expert", None),
        P("section", None, "expert"),
        P("section", None, "expert"),
        P("section", "expert", None),
    )
    return jax.shard_map(
        local,
        mesh=mesh,
        in_specs=placed,
        out_specs=(P("section", "rep", "expert", None), P("section", None)),
        check_vma=False,
    )
```

time: 103 us -> 57 us (0.55)
  blocking collectives: 47.6 us -> 0 us
  matrix products: 33 us -> 0 us
  Pallas kernels: 0 us -> 31 us
  starting transfers between devices: 8.58 us -> 15.7 us
  waiting for transfers between devices: 8.32 us -> 6.18 us
    psum x1 -> x0, blocking collectives: 40.2 us -> none  [local(): total_load = lax.psum(jnp.sum(gate_mass, axis=0), ('rep', 'expert'))]
    dot_general x5 -> x0, matrix products: 33 us -> none  [the longest x1 20.1 us: local(): partial_out = jnp.dot(hidden, down_w, preferred_element_type=jnp.float32)]
    pallas_call x0 -> x3, Pallas kernels: none -> 31 us  [the longest x1 29.3 us: local(): pl.pallas_call(functools.partial(expert_kernel, peers, depth, span, 4), o...]
    ppermute x1 -> x12, starting transfers between devices: 0.07 us -> 15.7 us  [the longest x4 8.24 us: local(): total = total + lax.ppermute(total, axis, route)]
    all_to_all x2 -> x0, starting transfers between devices: 8.51 us -> none  [the longest x1 5.19 us: local(): lax.all_to_all(copy_weights, 'expert', split_axis=0, concat_axis=0, tiled...]
    all_to_all x2 -> x0, waiting for transfers between devices: 8.32 us -> none  [the longest x1 4.84 us: local(): lax.all_to_all(copies, 'expert', split_axis=0, concat_axis=0, tiled=True)]
    all_to_all x1 -> x0, blocking collectives: 7.36 us -> none  [local(): lax.all_to_all(weighted, 'expert', split_axis=0, concat_axis=0, tiled=True)]
    ppermute x1 -> x12, waiting for transfers between devices: 0.01 us -> 6.18 us  [the longest x4 4.08 us: local(): total = total + lax.ppermute(total, axis, route)]
  transfers between devices with their start and end apart: 3 -> 12, of which waited for: 2 -> 3; matrix products, arithmetic and copies ran while one was open for 2% -> 1% of each run, Pallas kernels for 0% -> 52%
where the time goes in v1:
time: 57 us; the launch traced here: 56.7 us
  Pallas kernels  31 us (54%)
  starting transfers between devices  15.7 us (28%)
  waiting for transfers between devices  6.18 us (11%)
  local copies, waits for them, and re-layouts  2.54 us (4%)
  between operations  0.69 us (1%)
  other arithmetic  0.64 us (1%)
    pallas_call x1, Pallas kernels, local(): pl.pallas_call(functools.partial(expert_kernel, peers, depth, span, 4), o...  29.3 us
    ppermute x4, starting transfers between devices, local(): total = total + lax.ppermute(total, axis, route)  8.24 us
    ppermute x4, waiting for transfers between devices, local(): total = total + lax.ppermute(total, axis, route)  4.08 us
    ppermute x3, starting transfers between devices, local(): got[distance] = lax.ppermute(sent[distance], 'expert', route)  3.49 us
    ppermute x4, starting transfers between devices, local(): home[distance] = lax.ppermute(back[distance], ('section', 'expert'), route)  3.38 us
    unnamed x6, local copies, waits for them, and re-layouts  2.54 us
    ppermute x4, waiting for transfers between devices, local(): home[distance] = lax.ppermute(back[distance], ('section', 'expert'), route)  2.09 us
    pallas_call x1, Pallas kernels, local(): pl.pallas_call(functools.partial(combine_kernel, peers), out_shape=jax.Sh...  1.35 us
  transfers between devices with their start and end apart: 12, of which 3 were waited for; matrix products, arithmetic and copies ran while one was open for 1% of the time, Pallas kernels for 52%

profile of v1, /device:TPU:0, one launch (start us, length us, event | category | flops | bytes accessed | tf_op | source)
XLA Modules:
  0.0 56.7 jit_solution(8162055209729463246)
XLA Ops:
  0.6 0.0 copy-start
  0.6 1.2 %copy-done = bf16[1,1,64,7168]{3,2,1,0:T(8,128)(2,1)S(1)} copy-done((bf16[1,1,64,7168]{3,2,1,0:T(8,128)(2,1)S(1)}, bf16[1,1,64,7168]{3,2,1,0:T(8,128)(2,1)}, u32[]{:S(2)}) %copy-start) | copy-done | bytes 917528
  1.8 0.0 copy-start.1
  1.8 0.7 %copy-done.1 = s32[1,1,64,8]{2,3,1,0:T(8,128)S(1)} copy-done((s32[1,1,64,8]{2,3,1,0:T(8,128)S(1)}, s32[1,1,64,8]{2,3,1,0:T(8,128)}, u32[]{:S(2)}) %copy-start.1) | copy-done | bytes 2072
  2.5 0.0 copy-start.2
  2.5 0.7 %copy-done.2 = f32[1,1,64,8]{2,3,1,0:T(8,128)S(1)} copy-done((f32[1,1,64,8]{2,3,1,0:T(8,128)S(1)}, f32[1,1,64,8]{2,3,1,0:T(8,128)}, u32[]{:S(2)}) %copy-start.2) | copy-done | bytes 2072
  3.2 0.4 route.1
  3.6 0.6 collective-permute-start
  4.1 2.6 %collective-permute-start.8 = (f32[4,1]{1,0:T(4,128)S(1)}, f32[4,1]{1,0:T(4,128)S(1)}, u32[]{:S(2)}, u32[]{:S(2)}) collective-permute-start(f32[4,1]{1,0:T(4,128)S(1)} %bitcast.17), channel_id=1, source_target_pairs={{0,1},{1,0},{2,3},{3,2},{4,5},{5,4},{6,7},{7,6},{8,9},{9,8},{10,11... | collective-permute-start | bytes 56 | tf_op jit(solution)/shard_map/ppermute | solution.py:165
  6.7 0.1 collective-permute-start.1
  6.7 2.0 %collective-permute-start.2 = (bf16[2,7168]{1,0:T(2,128)(2,1)S(1)}, bf16[2,7168]{1,0:T(2,128)(2,1)S(1)}, u32[]{:S(2)}, u32[]{:S(2)}) collective-permute-start(bf16[2,7168]{1,0:T(2,128)(2,1)S(1)} %get-tuple-element.15), channel_id=1, source_target_pairs={{0,2},{1,3},{2,0},{3,1},{4,6},{5,7},{6,4},{7,5},{8,10},{9,11},{10,... | collective-permute-start | bytes 86024 | tf_op jit(solution)/shard_map/ppermute | solution.py:156
  8.7 1.4 %collective-permute-start.3 = (bf16[2,7168]{1,0:T(2,128)(2,1)S(1)}, bf16[2,7168]{1,0:T(2,128)(2,1)S(1)}, u32[]{:S(2)}, u32[]{:S(2)}) collective-permute-start(bf16[2,7168]{1,0:T(2,128)(2,1)S(1)} %get-tuple-element.16), channel_id=1, source_target_pairs={{0,3},{1,2},{2,1},{3,0},{4,7},{5,6},{6,5},{7,4},{8,11},{9,10},{10,... | collective-permute-start | bytes 86024 | tf_op jit(solution)/shard_map/ppermute | solution.py:156
  10.2 0.0 collective-permute-done.8
  10.2 1.5 %collective-permute-start.9 = (f32[4,1]{1,0:T(4,128)S(1)}, f32[4,1]{1,0:T(4,128)S(1)}, u32[]{:S(2)}, u32[]{:S(2)}) collective-permute-start(f32[4,1]{1,0:T(4,128)S(1)} %slice_add_fusion), channel_id=1, source_target_pairs={{0,2},{1,3},{2,0},{3,1},{4,6},{5,7},{6,4},{7,5},{8,10},{9,11},{10,... | collective-permute-start | bytes 56 | tf_op jit(solution)/shard_map/ppermute | solution.py:165
  11.7 2.1 %collective-permute-done.9 = f32[4,1]{1,0:T(4,128)S(1)} collective-permute-done((f32[4,1]{1,0:T(4,128)S(1)}, f32[4,1]{1,0:T(4,128)S(1)}, u32[]{:S(2)}, u32[]{:S(2)}) %collective-permute-start.9) | collective-permute-done | bytes 48 | tf_op jit(solution)/shard_map/ppermute | solution.py:165
  13.8 1.6 %collective-permute-start.10 = (f32[4,1]{1,0:T(4,128)S(1)}, f32[4,1]{1,0:T(4,128)S(1)}, u32[]{:S(2)}, u32[]{:S(2)}) collective-permute-start(f32[4,1]{1,0:T(4,128)S(1)} %add.13), channel_id=1, source_target_pairs={{0,4},{4,0},{8,12},{12,8},{1,5},{5,1},{9,13},{13,9},{2,6},{6,2},{1... | collective-permute-start | bytes 56 | tf_op jit(solution)/shard_map/ppermute | solution.py:165
  15.3 2.0 %collective-permute-done.10 = f32[4,1]{1,0:T(4,128)S(1)} collective-permute-done((f32[4,1]{1,0:T(4,128)S(1)}, f32[4,1]{1,0:T(4,128)S(1)}, u32[]{:S(2)}, u32[]{:S(2)}) %collective-permute-start.10) | collective-permute-done | bytes 48 | tf_op jit(solution)/shard_map/ppermute | solution.py:165
  17.3 2.6 %collective-permute-start.11 = (f32[4,1]{1,0:T(4,128)S(1)}, f32[4,1]{1,0:T(4,128)S(1)}, u32[]{:S(2)}, u32[]{:S(2)}) collective-permute-start(f32[4,1]{1,0:T(4,128)S(1)} %add.14), channel_id=1, source_target_pairs={{0,8},{4,12},{8,0},{12,4},{1,9},{5,13},{9,1},{13,5},{2,10},{6,14},... | collective-permute-start | bytes 56 | tf_op jit(solution)/shard_map/ppermute | solution.py:165
  19.9 0.0 collective-permute-done.1.refs_1_
  19.9 0.0 collective-permute-done.2.refs_2_
  19.9 0.0 collective-permute-done.3.refs_3_
  19.9 29.3 %expert.1 = (bf16[2,7168]{1,0:T(2,128)(2,1)S(1)}, bf16[2,7168]{1,0:T(2,128)(2,1)S(1)}, bf16[2,7168]{1,0:T(2,128)(2,1)S(1)}, bf16[2,7168]{1,0:T(2,128)(2,1)S(1)}) custom-call(bf16[2,7168]{1,0:T(2,128)(2,1)S(1)} %get-tuple-element.13.refs_0_, bf16[2,7168]{1,0:T(2,128)(2,1)S(1)} %collective-permute-done.1.refs_1_, ...), custom_call_target="tpu_custom_call" | custom-call | tf_op jit(solution)/shard_map/expert/pallas_call | solution.py:170
  49.3 0.1 collective-permute-start.4
  49.3 0.6 %collective-permute-start.5 = (bf16[2,7168]{1,0:T(2,128)(2,1)S(1)}, bf16[2,7168]{1,0:T(2,128)(2,1)S(1)}, u32[]{:S(2)}, u32[]{:S(2)}) collective-permute-start(bf16[2,7168]{1,0:T(2,128)(2,1)S(1)} %get-tuple-element.18), channel_id=1, source_target_pairs={{1,16},{0,17},{3,18},{2,19},{17,0},{16,1},{19,2},{18,3},{5,20},{4,... | collective-permute-start | bytes 86024 | tf_op jit(solution)/shard_map/ppermute | solution.py:195
  50.0 1.2 %collective-permute-start.6 = (bf16[2,7168]{1,0:T(2,128)(2,1)S(1)}, bf16[2,7168]{1,0:T(2,128)(2,1)S(1)}, u32[]{:S(2)}, u32[]{:S(2)}) collective-permute-start(bf16[2,7168]{1,0:T(2,128)(2,1)S(1)} %get-tuple-element.19), channel_id=1, source_target_pairs={{2,16},{3,17},{0,18},{1,19},{18,0},{19,1},{16,2},{17,3},{6,20},{7,... | collective-permute-start | bytes 86024 | tf_op jit(solution)/shard_map/ppermute | solution.py:195
  51.2 0.0 collective-permute-done.11
  51.2 1.5 %collective-permute-start.7 = (bf16[2,7168]{1,0:T(2,128)(2,1)S(1)}, bf16[2,7168]{1,0:T(2,128)(2,1)S(1)}, u32[]{:S(2)}, u32[]{:S(2)}) collective-permute-start(bf16[2,7168]{1,0:T(2,128)(2,1)S(1)} %get-tuple-element.20), channel_id=1, source_target_pairs={{3,16},{2,17},{1,18},{0,19},{19,0},{18,1},{17,2},{16,3},{7,20},{6,... | collective-permute-start | bytes 86024 | tf_op jit(solution)/shard_map/ppermute | solution.py:195
  52.6 0.6 %multiply_reduce_fusion = f32[4]{0:T(128)} fusion(f32[4,1]{1,0:T(4,128)S(1)} %add.14, f32[4,1]{1,0:T(4,128)S(1)} %collective-permute-done.11), kind=kLoop, calls=%fused_computation | loop fusion | flops 8 | bytes 48 | tf_op jit(solution)/shard_map/div | solution.py:204
  53.3 0.0 collective-permute-done.picks_ref
  53.3 0.0 collective-permute-done.4.refs_0_
  53.3 0.0 collective-permute-done.5.refs_1_
  53.3 0.0 collective-permute-done.6.refs_2_
  53.3 2.1 %collective-permute-done.7.refs_3_ = bf16[2,7168]{1,0:T(2,128)(2,1)S(1)} collective-permute-done((bf16[2,7168]{1,0:T(2,128)(2,1)S(1)}, bf16[2,7168]{1,0:T(2,128)(2,1)S(1)}, u32[]{:S(2)}, u32[]{:S(2)}) %collective-permute-start.7) | collective-permute-done | bytes 28704 | tf_op jit(solution)/shard_map/ppermute | solution.py:195
  55.4 1.3 %combine.1 = bf16[64,7168]{1,0:T(8,128)(2,1)} custom-call(bf16[8,64]{1,0:T(8,128)(2,1)S(1)} %collective-permute-done.picks_ref, bf16[2,7168]{1,0:T(2,128)(2,1)S(1)} %collective-permute-done.4.refs_0_, bf16[2,7168]{1,0:T(2,128)(2,1)S(1)} %collective-permute-done.5.refs_1_, bf16[2,7168]{1,0:T(2,128)(2,1)S(1)} %collective-permute-done.6.refs_2_, ...), custom_call_target="tpu_custom_call" | custom-call | tf_op jit(solution)/shard_map/combine/pallas_call | solution.py:196
  (3 shorter events, 0.0 us)
Async XLA Ops:
  0.6 1.2 %copy-start = (bf16[1,1,64,7168]{3,2,1,0:T(8,128)(2,1)S(1)}, bf16[1,1,64,7168]{3,2,1,0:T(8,128)(2,1)}, u32[]{:S(2)}) copy-start(bf16[1,1,64,7168]{3,2,1,0:T(8,128)(2,1)} %param.6) | copy-start | bytes 2752516
  1.8 0.7 %copy-start.1 = (s32[1,1,64,8]{2,3,1,0:T(8,128)S(1)}, s32[1,1,64,8]{2,3,1,0:T(8,128)}, u32[]{:S(2)}) copy-start(s32[1,1,64,8]{2,3,1,0:T(8,128)} %param.7) | copy-start | bytes 6148
  2.5 0.7 %copy-start.2 = (f32[1,1,64,8]{2,3,1,0:T(8,128)S(1)}, f32[1,1,64,8]{2,3,1,0:T(8,128)}, u32[]{:S(2)}) copy-start(f32[1,1,64,8]{2,3,1,0:T(8,128)} %param.8) | copy-start | bytes 6148
  3.6 49.7 %collective-permute-start = (bf16[8,64]{1,0:T(8,128)(2,1)S(1)}, bf16[8,64]{1,0:T(8,128)(2,1)S(1)}, u32[]{:S(2)}, u32[]{:S(2)}) collective-permute-start(bf16[8,64]{1,0:T(8,128)(2,1)S(1)} %get-tuple-element.12), channel_id=1, source_target_pairs={{0,16},{16,0},{1,17},{17,1},{2,18},{18,2},{3,19},{19,3},{4,20},{20... | collective-permute-start | bytes 3080 | tf_op jit(solution)/shard_map/ppermute | solution.py:158
  4.1 6.0 %collective-permute-start.8 = (f32[4,1]{1,0:T(4,128)S(1)}, f32[4,1]{1,0:T(4,128)S(1)}, u32[]{:S(2)}, u32[]{:S(2)}) collective-permute-start(f32[4,1]{1,0:T(4,128)S(1)} %bitcast.17), channel_id=1, source_target_pairs={{0,1},{1,0},{2,3},{3,2},{4,5},{5,4},{6,7},{7,6},{8,9},{9,8},{10,11... | collective-permute-start | bytes 56 | tf_op jit(solution)/shard_map/ppermute | solution.py:165
  6.7 13.3 %collective-permute-start.1 = (bf16[2,7168]{1,0:T(2,128)(2,1)S(1)}, bf16[2,7168]{1,0:T(2,128)(2,1)S(1)}, u32[]{:S(2)}, u32[]{:S(2)}) collective-permute-start(bf16[2,7168]{1,0:T(2,128)(2,1)S(1)} %get-tuple-element.14), channel_id=1, source_target_pairs={{0,1},{1,0},{2,3},{3,2},{4,5},{5,4},{6,7},{7,6},{8,9},{9,8},{10,11... | collective-permute-start | bytes 86024 | tf_op jit(solution)/shard_map/ppermute | solution.py:156
  6.7 13.2 %collective-permute-start.2 = (bf16[2,7168]{1,0:T(2,128)(2,1)S(1)}, bf16[2,7168]{1,0:T(2,128)(2,1)S(1)}, u32[]{:S(2)}, u32[]{:S(2)}) collective-permute-start(bf16[2,7168]{1,0:T(2,128)(2,1)S(1)} %get-tuple-element.15), channel_id=1, source_target_pairs={{0,2},{1,3},{2,0},{3,1},{4,6},{5,7},{6,4},{7,5},{8,10},{9,11},{10,... | collective-permute-start | bytes 86024 | tf_op jit(solution)/shard_map/ppermute | solution.py:156
  8.7 11.2 %collective-permute-start.3 = (bf16[2,7168]{1,0:T(2,128)(2,1)S(1)}, bf16[2,7168]{1,0:T(2,128)(2,1)S(1)}, u32[]{:S(2)}, u32[]{:S(2)}) collective-permute-start(bf16[2,7168]{1,0:T(2,128)(2,1)S(1)} %get-tuple-element.16), channel_id=1, source_target_pairs={{0,3},{1,2},{2,1},{3,0},{4,7},{5,6},{6,5},{7,4},{8,11},{9,10},{10,... | collective-permute-start | bytes 86024 | tf_op jit(solution)/shard_map/ppermute | solution.py:156
  10.2 3.6 %collective-permute-start.9 = (f32[4,1]{1,0:T(4,128)S(1)}, f32[4,1]{1,0:T(4,128)S(1)}, u32[]{:S(2)}, u32[]{:S(2)}) collective-permute-start(f32[4,1]{1,0:T(4,128)S(1)} %slice_add_fusion), channel_id=1, source_target_pairs={{0,2},{1,3},{2,0},{3,1},{4,6},{5,7},{6,4},{7,5},{8,10},{9,11},{10,... | collective-permute-start | bytes 56 | tf_op jit(solution)/shard_map/ppermute | solution.py:165
  13.8 3.6 %collective-permute-start.10 = (f32[4,1]{1,0:T(4,128)S(1)}, f32[4,1]{1,0:T(4,128)S(1)}, u32[]{:S(2)}, u32[]{:S(2)}) collective-permute-start(f32[4,1]{1,0:T(4,128)S(1)} %add.13), channel_id=1, source_target_pairs={{0,4},{4,0},{8,12},{12,8},{1,5},{5,1},{9,13},{13,9},{2,6},{6,2},{1... | collective-permute-start | bytes 56 | tf_op jit(solution)/shard_map/ppermute | solution.py:165
  17.3 33.8 %collective-permute-start.11 = (f32[4,1]{1,0:T(4,128)S(1)}, f32[4,1]{1,0:T(4,128)S(1)}, u32[]{:S(2)}, u32[]{:S(2)}) collective-permute-start(f32[4,1]{1,0:T(4,128)S(1)} %add.14), channel_id=1, source_target_pairs={{0,8},{4,12},{8,0},{12,4},{1,9},{5,13},{9,1},{13,5},{2,10},{6,14},... | collective-permute-start | bytes 56 | tf_op jit(solution)/shard_map/ppermute | solution.py:165
  49.3 4.0 %collective-permute-start.4 = (bf16[2,7168]{1,0:T(2,128)(2,1)S(1)}, bf16[2,7168]{1,0:T(2,128)(2,1)S(1)}, u32[]{:S(2)}, u32[]{:S(2)}) collective-permute-start(bf16[2,7168]{1,0:T(2,128)(2,1)S(1)} %get-tuple-element.17), channel_id=1, source_target_pairs={{0,16},{1,17},{2,18},{3,19},{16,0},{17,1},{18,2},{19,3},{4,20},{5,... | collective-permute-start | bytes 86024 | tf_op jit(solution)/shard_map/ppermute | solution.py:195
  49.3 4.0 %collective-permute-start.5 = (bf16[2,7168]{1,0:T(2,128)(2,1)S(1)}, bf16[2,7168]{1,0:T(2,128)(2,1)S(1)}, u32[]{:S(2)}, u32[]{:S(2)}) collective-permute-start(bf16[2,7168]{1,0:T(2,128)(2,1)S(1)} %get-tuple-element.18), channel_id=1, source_target_pairs={{1,16},{0,17},{3,18},{2,19},{17,0},{16,1},{19,2},{18,3},{5,20},{4,... | collective-permute-start | bytes 86024 | tf_op jit(solution)/shard_map/ppermute | solution.py:195
  50.0 3.3 %collective-permute-start.6 = (bf16[2,7168]{1,0:T(2,128)(2,1)S(1)}, bf16[2,7168]{1,0:T(2,128)(2,1)S(1)}, u32[]{:S(2)}, u32[]{:S(2)}) collective-permute-start(bf16[2,7168]{1,0:T(2,128)(2,1)S(1)} %get-tuple-element.19), channel_id=1, source_target_pairs={{2,16},{3,17},{0,18},{1,19},{18,0},{19,1},{16,2},{17,3},{6,20},{7,... | collective-permute-start | bytes 86024 | tf_op jit(solution)/shard_map/ppermute | solution.py:195
  51.2 4.2 %collective-permute-start.7 = (bf16[2,7168]{1,0:T(2,128)(2,1)S(1)}, bf16[2,7168]{1,0:T(2,128)(2,1)S(1)}, u32[]{:S(2)}, u32[]{:S(2)}) collective-permute-start(bf16[2,7168]{1,0:T(2,128)(2,1)S(1)} %get-tuple-element.20), channel_id=1, source_target_pairs={{3,16},{2,17},{1,18},{0,19},{19,0},{18,1},{17,2},{16,3},{7,20},{6,... | collective-permute-start | bytes 86024 | tf_op jit(solution)/shard_map/ppermute | solution.py:195
